TPU v7x, 32 devices: a whole 2x2x4 slice. The times are simulated.
32 devices in a mesh: ord: 8 (over z, core), gx: 2 (over x), gy: 2 (over y).
Axes of the slice: x: 2, y: 2, z: 4, core: 2. Of those that a mesh axis runs over, the one named last changes fastest.
Arguments:
- distribution: float32 [256, 64, 8, 128], P('ord', 'gx', 'gy'), may hold values from -4.5 to 4.5
- relaxation: float32 [64, 8, 128], P('gx', 'gy'), may hold values from 0.05 to 5
Outputs:
- updated: float32 [256, 64, 8, 128], P('ord', 'gx', 'gy')
- temperature: float32 [64, 8, 128], P('gx', 'gy')
All inputs are finite; a program needn't handle non-finite values.
Results may differ from a plain program's by a relative error of at most 0.0003.
Values sent between devices are 32-bit elements; how exact they have to be, the bound alone decides.
A program may use at most 64 MiB of HBM per device.

v0:
```python
import jax
import jax.numpy as jnp
from jax import lax
from jax.sharding import PartitionSpec as P

NORD = 256
STEPS = 2
SWEEPS = 3
time_step = 0.4
limiter_eps = 0.01
diffusion_mass = 0.5
flux_weight = 2.0
golden_turn = 2.399963229728653


def extended(cells, sides, width):
    for axis, dim in sides:
        count = lax.axis_size(axis)
        ends = count - 1
        head = lax.slice_in_dim(cells, 0, width, axis=dim)
        tail = lax.slice_in_dim(cells, cells.shape[dim] - width, cells.shape[dim], axis=dim)
        cells = jnp.concatenate(
            [
                lax.ppermute(tail, axis, [(i, (i + 1) % count) for i in range(ends)]),
                cells,
                lax.ppermute(head, axis, [((i + 1) % count, i) for i in range(ends)]),
            ],
            axis=dim,
        )
    return cells


def directions(offset, length):
    ordinal = (offset + jnp.arange(length, dtype=jnp.int32)).astype(jnp.float32)
    height = 1.0 - (2.0 * ordinal + 1.0) / NORD
    radius = jnp.sqrt(1.0 - height * height)
    turned = golden_turn * ordinal
    return jnp.stack([radius * jnp.cos(turned), radius * jnp.sin(turned), height])


def window(values, anchor, length, axis_dim):
    return lax.slice_in_dim(values, anchor, anchor + length, axis=axis_dim)


def pad_along(values, width, axis_dim):
    widths = [
        (width, width) if dimension == axis_dim else (0, 0) for dimension in range(values.ndim)
    ]
    return jnp.pad(values, widths)


def source_of(current, local_temp, relax):
    return ((2.0 * relax - time_step) * current + 2.0 * time_step * local_temp) / (
        2.0 * relax + time_step
    )


def axis_flux(padded, temp_pad, relax_pad, along_speed, axis_dim):
    length = padded.shape[axis_dim] - 4
    lower_diff = window(padded, 1, length + 2, axis_dim) - window(padded, 0, length + 2, axis_dim)
    upper_diff = window(padded, 2, length + 2, axis_dim) - window(padded, 1, length + 2, axis_dim)
    centre = window(padded, 1, length + 2, axis_dim)
    slopes = (
        lower_diff * (upper_diff * upper_diff + limiter_eps)
        + upper_diff * (lower_diff * lower_diff + limiter_eps)
    ) / (lower_diff * lower_diff + upper_diff * upper_diff + 2.0 * limiter_eps)
    upwind_low = window(centre, 0, length + 1, axis_dim) + 0.5 * (
        1.0 - time_step * along_speed
    ) * window(slopes, 0, length + 1, axis_dim)
    upwind_high = window(centre, 1, length + 1, axis_dim) - 0.5 * (
        1.0 + time_step * along_speed
    ) * window(slopes, 1, length + 1, axis_dim)
    upwind = jnp.where(along_speed >= 0.0, upwind_low, upwind_high)
    temp_face = 0.5 * (
        window(temp_pad, 0, length + 1, axis_dim) + window(temp_pad, 1, length + 1, axis_dim)
    )
    relax_face = 0.5 * (
        window(relax_pad, 0, length + 1, axis_dim) + window(relax_pad, 1, length + 1, axis_dim)
    )
    edges = (2.0 * relax_face * upwind + 0.5 * time_step * temp_face) / (
        2.0 * relax_face + 0.5 * time_step
    )
    return along_speed * (window(edges, 1, length, axis_dim) - window(edges, 0, length, axis_dim))


def spread(flux_x_pad, flux_y_pad, flux_z):
    flux_z_pad = jnp.pad(flux_z, ((0, 0), (0, 0), (1, 1)))
    result = 0.5 * (flux_x_pad[2:, 1:-1, 1:-1] - flux_x_pad[:-2, 1:-1, 1:-1])
    result = result + 0.5 * (flux_y_pad[1:-1, 2:, 1:-1] - flux_y_pad[1:-1, :-2, 1:-1])
    return result + 0.5 * (flux_z_pad[:, :, 2:] - flux_z_pad[:, :, :-2])


def relax_sweep(potential_pad, driver):
    conduct = 1.0 / (1.0 + potential_pad * potential_pad)
    centre = conduct[1:-1, 1:-1, 1:-1]
    weighted = diffusion_mass * driver
    weights = diffusion_mass + jnp.zeros_like(driver)
    for axis_dim in range(3):
        for anchor in (0, 2):
            picker = tuple(
                (
                    (
                        slice(anchor, anchor + potential_pad.shape[axis_dim] - 2)
                        if dimension == axis_dim
                        else slice(1, -1)
                    )
                    for dimension in range(3)
                )
            )
            couple = 0.5 * (centre + conduct[picker])
            weighted = weighted + couple * potential_pad[picker]
            weights = weights + couple
    return weighted / weights


def transport(current, local_temp, relax, speeds):
    source = source_of(current, local_temp, relax)
    ordinal_rows = source.shape[0]
    stacked = jnp.concatenate([source, local_temp[None], relax[None]], 0)
    widened = extended(stacked, (("gx", 1), ("gy", 2)), 2)
    along_x = widened[:, :, 2:-2, :]
    along_y = widened[:, 2:-2, :, :]
    fluxes = axis_flux(
        along_x[:ordinal_rows],
        along_x[ordinal_rows : ordinal_rows + 1, 1:-1],
        along_x[ordinal_rows + 1 :, 1:-1],
        speeds[0][:, None, None, None],
        1,
    )
    fluxes = fluxes + axis_flux(
        along_y[:ordinal_rows],
        along_y[ordinal_rows : ordinal_rows + 1, :, 1:-1],
        along_y[ordinal_rows + 1 :, :, 1:-1],
        speeds[1][:, None, None, None],
        2,
    )
    fluxes = fluxes + axis_flux(
        pad_along(source, 2, 3),
        pad_along(local_temp[None], 1, 3),
        pad_along(relax[None], 1, 3),
        speeds[2][:, None, None, None],
        3,
    )
    return source - time_step * fluxes


def block_extend(stacked):
    widened = extended(stacked, (("gx", 1), ("gy", 2)), 1)
    return jnp.pad(widened, ((0, 0), (0, 0), (0, 0), (1, 1)))


def diffuse(shares, extend):
    energy = shares[0]
    widened = extend(shares[:3])
    driver = energy - flux_weight * spread(widened[1], widened[2], shares[3])
    potential = relax_sweep(widened[0], driver)
    for rounds in range(1, SWEEPS):
        potential = relax_sweep(extend(potential[None])[0], driver)
    return potential


def local(distribution, relaxation):
    local_count = distribution.shape[0]
    speeds = directions(lax.axis_index("ord") * local_count, local_count)
    current = distribution
    for repeat in range(STEPS):
        local_temp = lax.psum(jnp.sum(current, 0) / NORD, "ord")
        current = transport(current, local_temp, relaxation, speeds)
    partial_value = (
        jnp.concatenate(
            [jnp.sum(current, 0)[None], jnp.sum(speeds[:, :, None, None, None] * current[None], 1)],
            0,
        )
        / NORD
    )
    shares = lax.psum(partial_value, "ord")
    potential = diffuse(shares, block_extend)
    updated = source_of(current, potential, relaxation)
    return (updated, potential)


def solution(mesh):
    placed = (P("ord", "gx", "gy", None), P("gx", "gy", None))
    return jax.shard_map(
        local,
        mesh=mesh,
        in_specs=placed,
        out_specs=(P("ord", "gx", "gy", None), P("gx", "gy", None)),
        check_vma=False,
    )
```

profile of v0, /device:TPU:0, one launch (start us, length us, event | category | flops | bytes accessed | tf_op | source)
XLA Modules:
  0.0 365.7 jit_solution(15019233585724942882)
XLA Ops:
  7.2 2.0 reduce_sum.36
  12.2 56.1 %all-reduce.13.cloned.1.call-done = f32[32,4,128]{2,1,0:T(4,128)} async-done(((f32[32,4,128]{2,1,0:T(4,128)}), f32[32,4,128]{2,1,0:T(4,128)}) %all-reduce.13.cloned.1.call-update) | async-done | bytes 65552 | tf_op jit(solution)/shard_map/psum | solution.py:167
  71.5 2.4 add_divide_fusion.1
  74.3 3.4 collective-permute-start
  79.0 2.6 fusion.4
  81.5 3.0 collective-permute-done.1
  85.2 3.5 collective-permute-start.2
  88.7 1.5 collective-permute-start.3
  92.2 1.4 fusion.66
  93.6 21.6 %collective-permute-done.2 = f32[34,36,2,128]{3,1,2,0:T(8,128)S(1)} collective-permute-done((f32[34,36,2,128]{3,1,2,0:T(8,128)S(1)}, f32[34,36,2,128]{3,1,2,0:T(8,128)S(1)}, u32[]{:S(2)}, u32[]{:S(2)}) %collective-permute-start.2) | collective-permute-done | bytes 1253408 | tf_op jit(solution)/shard_map/ppermute | solution.py:24
  115.3 4.2 %collective-permute-done.3 = f32[34,36,2,128]{3,1,2,0:T(8,128)S(1)} collective-permute-done((f32[34,36,2,128]{3,1,2,0:T(8,128)S(1)}, f32[34,36,2,128]{3,1,2,0:T(8,128)S(1)}, u32[]{:S(2)}, u32[]{:S(2)}) %collective-permute-start.3) | collective-permute-done | bytes 1253408 | tf_op jit(solution)/shard_map/ppermute | solution.py:26
  119.5 3.6 fusion.18
  123.1 3.5 add_divide_fusion.3
  126.6 1.8 fusion.60
  128.4 1.8 fusion.158
  131.0 53.0 %all-reduce.15.cloned.1.call-done = f32[32,4,128]{2,1,0:T(4,128)} async-done(((f32[32,4,128]{2,1,0:T(4,128)}), f32[32,4,128]{2,1,0:T(4,128)}) %all-reduce.15.cloned.1.call-update) | async-done | bytes 65552 | tf_op jit(solution)/shard_map/psum | solution.py:167
  187.1 2.4 add_divide_fusion
  189.8 3.4 collective-permute-start.4
  193.2 1.5 collective-permute-start.5
  194.8 2.6 fusion.12
  197.4 2.8 collective-permute-done.5
  200.8 3.5 collective-permute-start.6
  204.3 1.3 collective-permute-start.7
  207.6 1.4 fusion.54
  209.1 21.8 %collective-permute-done.6 = f32[34,36,2,128]{3,1,2,0:T(8,128)S(1)} collective-permute-done((f32[34,36,2,128]{3,1,2,0:T(8,128)S(1)}, f32[34,36,2,128]{3,1,2,0:T(8,128)S(1)}, u32[]{:S(2)}, u32[]{:S(2)}) %collective-permute-start.6) | collective-permute-done | bytes 1253408 | tf_op jit(solution)/shard_map/ppermute | solution.py:24
  230.9 4.2 %collective-permute-done.7 = f32[34,36,2,128]{3,1,2,0:T(8,128)S(1)} collective-permute-done((f32[34,36,2,128]{3,1,2,0:T(8,128)S(1)}, f32[34,36,2,128]{3,1,2,0:T(8,128)S(1)}, u32[]{:S(2)}, u32[]{:S(2)}) %collective-permute-start.7) | collective-permute-done | bytes 1253408 | tf_op jit(solution)/shard_map/ppermute | solution.py:26
  235.1 3.6 fusion.21
  238.7 3.5 add_divide_fusion.2
  242.2 1.7 fusion.48
  243.9 1.8 fusion.156
  245.8 1.3 copy-done.2
  248.7 53.9 %all-reduce.17.cloned.1.call-done = f32[4,32,4,128]{3,2,1,0:T(4,128)} async-done(((f32[4,32,4,128]{3,2,1,0:T(4,128)}), f32[4,32,4,128]{3,2,1,0:T(4,128)}) %all-reduce.17.cloned.1.call-update) | async-done | bytes 262160 | tf_op jit(solution)/shard_map/psum | solution.py:176
  303.2 3.4 collective-permute-start.8
  308.9 3.3 collective-permute-done.9
  312.2 3.4 collective-permute-start.10
  315.6 1.6 collective-permute-start.11
  318.0 3.6 collective-permute-done.11
  322.5 1.6 fusion.147
  324.1 1.6 collective-permute-start.12
  327.1 4.2 %collective-permute-done.13 = f32[1,1,4,128]{3,2,1,0:T(4,128)S(1)} collective-permute-done((f32[1,1,4,128]{3,2,1,0:T(4,128)S(1)}, f32[1,1,4,128]{3,2,1,0:T(4,128)S(1)}, u32[]{:S(2)}, u32[]{:S(2)}) %collective-permute-start.13) | collective-permute-done | bytes 2080 | tf_op jit(solution)/shard_map/ppermute | solution.py:26
  331.3 1.6 collective-permute-start.14
  334.3 4.2 %collective-permute-done.15 = f32[1,34,1,128]{3,2,1,0:T(1,128)S(1)} collective-permute-done((f32[1,34,1,128]{3,2,1,0:T(1,128)S(1)}, f32[1,34,1,128]{3,2,1,0:T(1,128)S(1)}, u32[]{:S(2)}, u32[]{:S(2)}) %collective-permute-start.15) | collective-permute-done | bytes 17440 | tf_op jit(solution)/shard_map/ppermute | solution.py:26
  339.6 1.7 collective-permute-start.16
  342.6 4.2 %collective-permute-done.17 = f32[1,1,4,128]{3,2,1,0:T(4,128)S(1)} collective-permute-done((f32[1,1,4,128]{3,2,1,0:T(4,128)S(1)}, f32[1,1,4,128]{3,2,1,0:T(4,128)S(1)}, u32[]{:S(2)}, u32[]{:S(2)}) %collective-permute-start.17) | collective-permute-done | bytes 2080 | tf_op jit(solution)/shard_map/ppermute | solution.py:26
  346.8 1.6 collective-permute-start.18
  348.4 1.3 collective-permute-start.19
  349.8 4.2 %collective-permute-done.19 = f32[1,34,1,128]{3,2,1,0:T(1,128)S(1)} collective-permute-done((f32[1,34,1,128]{3,2,1,0:T(1,128)S(1)}, f32[1,34,1,128]{3,2,1,0:T(1,128)S(1)}, u32[]{:S(2)}, u32[]{:S(2)}) %collective-permute-start.19) | collective-permute-done | bytes 17440 | tf_op jit(solution)/shard_map/ppermute | solution.py:26
  356.1 3.1 copy.53
  (94 shorter events, 30.8 us)
Async XLA Ops:
  7.2 63.9 %copy-start = (f32[32,32,4,128]{3,2,1,0:T(4,128)S(1)}, f32[32,32,4,128]{3,2,1,0:T(4,128)}, u32[]{:S(2)}) copy-start(f32[32,32,4,128]{3,2,1,0:T(4,128)} %param.2) | copy-start | bytes 6291460
  7.2 61.1 %all-reduce.13.cloned.1.call-start = ((), (), s32[]{:S(2)}) async-start(), calls=%async_computation | async-start | bytes 131072 | tf_op jit(solution)/shard_map/psum | solution.py:167
  9.9 174.1 %all-reduce.15.cloned.1.call-start = ((), (), s32[]{:S(2)}) async-start(), calls=%async_computation.1 | async-start | bytes 131072 | tf_op jit(solution)/shard_map/psum | solution.py:167
  74.3 7.3 %collective-permute-start = (f32[34,2,4,128]{3,1,2,0:T(2,128)S(1)}, f32[34,2,4,128]{3,1,2,0:T(2,128)S(1)}, u32[]{:S(2)}, u32[]{:S(2)}) collective-permute-start(f32[34,2,4,128]{3,1,2,0:T(2,128)S(1)} %get-tuple-element.44), channel_id=1, source_target_pairs={{0,2},{1,3},{4,6},{5,7},{8,10},{9,11},{12,14},{13,15},{16,18},{17,... | collective-permute-start | bytes 417800 | tf_op jit(solution)/shard_map/ppermute | solution.py:24
  77.6 6.9 %collective-permute-start.1 = (f32[34,2,4,128]{3,1,2,0:T(2,128)S(1)}, f32[34,2,4,128]{3,1,2,0:T(2,128)S(1)}, u32[]{:S(2)}, u32[]{:S(2)}) collective-permute-start(f32[34,2,4,128]{3,1,2,0:T(2,128)S(1)} %get-tuple-element.45), channel_id=1, source_target_pairs={{2,0},{3,1},{6,4},{7,5},{10,8},{11,9},{14,12},{15,13},{18,16},{19,... | collective-permute-start | bytes 417800 | tf_op jit(solution)/shard_map/ppermute | solution.py:26
  85.2 30.0 %collective-permute-start.2 = (f32[34,36,2,128]{3,1,2,0:T(8,128)S(1)}, f32[34,36,2,128]{3,1,2,0:T(8,128)S(1)}, u32[]{:S(2)}, u32[]{:S(2)}) collective-permute-start(f32[34,36,2,128]{3,1,2,0:T(8,128)S(1)} %get-tuple-element.33), channel_id=1, source_target_pairs={{0,1},{2,3},{4,5},{6,7},{8,9},{10,11},{12,13},{14,15},{16,17},{18,... | collective-permute-start | bytes 3760136 | tf_op jit(solution)/shard_map/ppermute | solution.py:24
  88.7 30.7 %collective-permute-start.3 = (f32[34,36,2,128]{3,1,2,0:T(8,128)S(1)}, f32[34,36,2,128]{3,1,2,0:T(8,128)S(1)}, u32[]{:S(2)}, u32[]{:S(2)}) collective-permute-start(f32[34,36,2,128]{3,1,2,0:T(8,128)S(1)} %get-tuple-element.32), channel_id=1, source_target_pairs={{1,0},{3,2},{5,4},{7,6},{9,8},{11,10},{13,12},{15,14},{17,16},{19,... | collective-permute-start | bytes 3760136 | tf_op jit(solution)/shard_map/ppermute | solution.py:26
  126.6 1.8 copy-start.1
  130.9 171.6 %all-reduce.17.cloned.1.call-start = ((), (), s32[]{:S(2)}) async-start(), calls=%async_computation.2 | async-start | bytes 524288 | tf_op jit(solution)/shard_map/psum | solution.py:176
  189.8 7.5 %collective-permute-start.4 = (f32[34,2,4,128]{3,1,2,0:T(2,128)S(1)}, f32[34,2,4,128]{3,1,2,0:T(2,128)S(1)}, u32[]{:S(2)}, u32[]{:S(2)}) collective-permute-start(f32[34,2,4,128]{3,1,2,0:T(2,128)S(1)} %get-tuple-element.40), channel_id=1, source_target_pairs={{0,2},{1,3},{4,6},{5,7},{8,10},{9,11},{12,14},{13,15},{16,18},{17,... | collective-permute-start | bytes 417800 | tf_op jit(solution)/shard_map/ppermute | solution.py:24
  193.2 6.9 %collective-permute-start.5 = (f32[34,2,4,128]{3,1,2,0:T(2,128)S(1)}, f32[34,2,4,128]{3,1,2,0:T(2,128)S(1)}, u32[]{:S(2)}, u32[]{:S(2)}) collective-permute-start(f32[34,2,4,128]{3,1,2,0:T(2,128)S(1)} %get-tuple-element.41), channel_id=1, source_target_pairs={{2,0},{3,1},{6,4},{7,5},{10,8},{11,9},{14,12},{15,13},{18,16},{19,... | collective-permute-start | bytes 417800 | tf_op jit(solution)/shard_map/ppermute | solution.py:26
  200.8 30.0 %collective-permute-start.6 = (f32[34,36,2,128]{3,1,2,0:T(8,128)S(1)}, f32[34,36,2,128]{3,1,2,0:T(8,128)S(1)}, u32[]{:S(2)}, u32[]{:S(2)}) collective-permute-start(f32[34,36,2,128]{3,1,2,0:T(8,128)S(1)} %get-tuple-element.31), channel_id=1, source_target_pairs={{0,1},{2,3},{4,5},{6,7},{8,9},{10,11},{12,13},{14,15},{16,17},{18,... | collective-permute-start | bytes 3760136 | tf_op jit(solution)/shard_map/ppermute | solution.py:24
  204.3 30.7 %collective-permute-start.7 = (f32[34,36,2,128]{3,1,2,0:T(8,128)S(1)}, f32[34,36,2,128]{3,1,2,0:T(8,128)S(1)}, u32[]{:S(2)}, u32[]{:S(2)}) collective-permute-start(f32[34,36,2,128]{3,1,2,0:T(8,128)S(1)} %get-tuple-element.30), channel_id=1, source_target_pairs={{1,0},{3,2},{5,4},{7,6},{9,8},{11,10},{13,12},{15,14},{17,16},{19,... | collective-permute-start | bytes 3760136 | tf_op jit(solution)/shard_map/ppermute | solution.py:26
  245.8 1.3 copy-start.2
  303.2 5.6 %collective-permute-start.8 = (f32[3,1,4,128]{3,2,1,0:T(4,128)S(1)}, f32[3,1,4,128]{3,2,1,0:T(4,128)S(1)}, u32[]{:S(2)}, u32[]{:S(2)}) collective-permute-start(f32[3,1,4,128]{3,2,1,0:T(4,128)S(1)} %get-tuple-element.49), channel_id=1, source_target_pairs={{0,2},{1,3},{4,6},{5,7},{8,10},{9,11},{12,14},{13,15},{16,18},{17,... | collective-permute-start | bytes 18440 | tf_op jit(solution)/shard_map/ppermute | solution.py:24
  306.6 5.5 %collective-permute-start.9 = (f32[3,1,4,128]{3,2,1,0:T(4,128)S(1)}, f32[3,1,4,128]{3,2,1,0:T(4,128)S(1)}, u32[]{:S(2)}, u32[]{:S(2)}) collective-permute-start(f32[3,1,4,128]{3,2,1,0:T(4,128)S(1)} %get-tuple-element.50), channel_id=1, source_target_pairs={{2,0},{3,1},{6,4},{7,5},{10,8},{11,9},{14,12},{15,13},{18,16},{19,... | collective-permute-start | bytes 18440 | tf_op jit(solution)/shard_map/ppermute | solution.py:26
  312.2 5.8 %collective-permute-start.10 = (f32[3,34,1,128]{3,2,1,0:T(1,128)S(1)}, f32[3,34,1,128]{3,2,1,0:T(1,128)S(1)}, u32[]{:S(2)}, u32[]{:S(2)}) collective-permute-start(f32[3,34,1,128]{3,2,1,0:T(1,128)S(1)} %get-tuple-element.51), channel_id=1, source_target_pairs={{0,1},{2,3},{4,5},{6,7},{8,9},{10,11},{12,13},{14,15},{16,17},{18,... | collective-permute-start | bytes 156680 | tf_op jit(solution)/shard_map/ppermute | solution.py:24
  315.6 6.0 %collective-permute-start.11 = (f32[3,34,1,128]{3,2,1,0:T(1,128)S(1)}, f32[3,34,1,128]{3,2,1,0:T(1,128)S(1)}, u32[]{:S(2)}, u32[]{:S(2)}) collective-permute-start(f32[3,34,1,128]{3,2,1,0:T(1,128)S(1)} %get-tuple-element.52), channel_id=1, source_target_pairs={{1,0},{3,2},{5,4},{7,6},{9,8},{11,10},{13,12},{15,14},{17,16},{19,... | collective-permute-start | bytes 156680 | tf_op jit(solution)/shard_map/ppermute | solution.py:26
  322.5 33.3 %copy-start.3 = (f32[32,32,4,128]{3,1,2,0:T(8,128)S(1)}, f32[32,32,4,128]{3,1,2,0:T(8,128)}, u32[]{:S(2)}) copy-start(f32[32,32,4,128]{3,1,2,0:T(8,128)} %copy-done.2) | copy-start | bytes 6291460
  324.1 3.0 collective-permute-start.12
  325.8 5.5 %collective-permute-start.13 = (f32[1,1,4,128]{3,2,1,0:T(4,128)S(1)}, f32[1,1,4,128]{3,2,1,0:T(4,128)S(1)}, u32[]{:S(2)}, u32[]{:S(2)}) collective-permute-start(f32[1,1,4,128]{3,2,1,0:T(4,128)S(1)} %get-tuple-element.60), channel_id=1, source_target_pairs={{2,0},{3,1},{6,4},{7,5},{10,8},{11,9},{14,12},{15,13},{18,16},{19,... | collective-permute-start | bytes 6152 | tf_op jit(solution)/shard_map/ppermute | solution.py:26
  331.3 3.0 collective-permute-start.14
  332.9 5.6 %collective-permute-start.15 = (f32[1,34,1,128]{3,2,1,0:T(1,128)S(1)}, f32[1,34,1,128]{3,2,1,0:T(1,128)S(1)}, u32[]{:S(2)}, u32[]{:S(2)}) collective-permute-start(f32[1,34,1,128]{3,2,1,0:T(1,128)S(1)} %get-tuple-element.56), channel_id=1, source_target_pairs={{1,0},{3,2},{5,4},{7,6},{9,8},{11,10},{13,12},{15,14},{17,16},{19,... | collective-permute-start | bytes 52232 | tf_op jit(solution)/shard_map/ppermute | solution.py:26
  339.6 3.0 collective-permute-start.16
  341.2 5.5 %collective-permute-start.17 = (f32[1,1,4,128]{3,2,1,0:T(4,128)S(1)}, f32[1,1,4,128]{3,2,1,0:T(4,128)S(1)}, u32[]{:S(2)}, u32[]{:S(2)}) collective-permute-start(f32[1,1,4,128]{3,2,1,0:T(4,128)S(1)} %get-tuple-element.58), channel_id=1, source_target_pairs={{2,0},{3,1},{6,4},{7,5},{10,8},{11,9},{14,12},{15,13},{18,16},{19,... | collective-permute-start | bytes 6152 | tf_op jit(solution)/shard_map/ppermute | solution.py:26
  346.8 3.1 collective-permute-start.18
  348.4 5.6 %collective-permute-start.19 = (f32[1,34,1,128]{3,2,1,0:T(1,128)S(1)}, f32[1,34,1,128]{3,2,1,0:T(1,128)S(1)}, u32[]{:S(2)}, u32[]{:S(2)}) collective-permute-start(f32[1,34,1,128]{3,2,1,0:T(1,128)S(1)} %get-tuple-element.54), channel_id=1, source_target_pairs={{1,0},{3,2},{5,4},{7,6},{9,8},{11,10},{13,12},{15,14},{17,16},{19,... | collective-permute-start | bytes 52232 | tf_op jit(solution)/shard_map/ppermute | solution.py:26
Sparse Core Ops, SparseCore 0:
  10.9 57.4 all-reduce.12
  131.0 52.9 all-reduce.14
  248.8 53.7 all-reduce.16
where the time goes:
time: 367 us; the launch traced here: 366 us
  waiting for transfers between devices  245 us (67%)
  other arithmetic  55.6 us (15%)
  starting transfers between devices  40.7 us (11%)
  between operations  14.5 us (4%)
  local copies, waits for them, and re-layouts  10.4 us (3%)
    psum x2, waiting for transfers between devices, local(): local_temp = lax.psum(jnp.sum(current, 0) / NORD, 'ord')  109 us
    psum x1, waiting for transfers between devices, local(): shares = lax.psum(partial_value, 'ord')  53.9 us
    ppermute x10, waiting for transfers between devices, extended(): lax.ppermute(tail, axis, [(i, (i + 1) % count) for i in range(ends)])  43.7 us
    ppermute x10, waiting for transfers between devices, extended(): lax.ppermute(head, axis, [((i + 1) % count, i) for i in range(ends)])  37.9 us
    ppermute x10, starting transfers between devices, extended(): lax.ppermute(tail, axis, [(i, (i + 1) % count) for i in range(ends)])  27 us
    div x6, other arithmetic, axis_flux(): (lower_diff * (upper_diff * upper_diff + limiter_eps) + upper_diff * (low...  14.3 us
    ppermute x10, starting transfers between devices, extended(): lax.ppermute(head, axis, [((i + 1) % count, i) for i in range(ends)])  13.6 us
    div x6, other arithmetic, axis_flux(): (2.0 * relax_face * upwind + 0.5 * time_step * temp_face) / (2.0 * relax_...  11.4 us
  transfers between devices with their start and end apart: 23, of which 17 were waited for; matrix products, arithmetic and copies ran while one was open for 4% of the time, Pallas kernels for 0%

commit v1 on v0

--- a/solution.py
+++ b/solution.py
@@ -173,7 +173,19 @@
         )
         / NORD
     )
-    shares = lax.psum(partial_value, "ord")
+
+    def _extend_skins(raw):
+        lane_axis = "ord"
+        carry = raw
+        amount_of = lax.axis_size(lane_axis)
+        for p in [
+            [(t, t ^ i0) for t in range(amount_of)] for i0 in (1, 2, 4, 8, 16) if i0 < amount_of
+        ]:
+            tall = lax.ppermute(carry, axis_name=lane_axis, perm=p)
+            carry = carry + tall
+        return carry
+
+    shares = _extend_skins(partial_value)
     potential = diffuse(shares, block_extend)
     updated = source_of(current, potential, relaxation)
     return (updated, potential)

time: 367 us -> 331 us (0.902)
  waiting for transfers between devices: 245 us -> 215 us
  local copies, waits for them, and re-layouts: 10.4 us -> 6.56 us
    psum x1 -> x0, waiting for transfers between devices: 53.9 us -> none  [local(): shares = lax.psum(partial_value, 'ord')]
    ppermute x0 -> x3, waiting for transfers between devices: none -> 21.8 us  [_extend_skins(): tall = lax.ppermute(carry, axis_name=lane_axis, perm=p)]
  transfers between devices with their start and end apart: 23 -> 25, of which waited for: 17 -> 19; matrix products, arithmetic and copies ran while one was open for 4% -> 4% of each run, Pallas kernels for 0% -> 0%
where the time goes in v1:
time: 331 us; the launch traced here: 330 us
  waiting for transfers between devices  215 us (65%)
  other arithmetic  54.1 us (16%)
  starting transfers between devices  40 us (12%)
  between operations  14.8 us (4%)
  local copies, waits for them, and re-layouts  6.56 us (2%)
    psum x2, waiting for transfers between devices, local(): local_temp = lax.psum(jnp.sum(current, 0) / NORD, 'ord')  109 us
    ppermute x10, waiting for transfers between devices, extended(): lax.ppermute(tail, axis, [(i, (i + 1) % count) for i in range(ends)])  44 us
    ppermute x10, waiting for transfers between devices, extended(): lax.ppermute(head, axis, [((i + 1) % count, i) for i in range(ends)])  39.6 us
    ppermute x10, starting transfers between devices, extended(): lax.ppermute(tail, axis, [(i, (i + 1) % count) for i in range(ends)])  24.3 us
    ppermute x3, waiting for transfers between devices, _extend_skins(): tall = lax.ppermute(carry, axis_name=lane_axis, perm=p)  21.8 us
    div x6, other arithmetic, axis_flux(): (lower_diff * (upper_diff * upper_diff + limiter_eps) + upper_diff * (low...  14.3 us
    ppermute x10, starting transfers between devices, extended(): lax.ppermute(head, axis, [((i + 1) % count, i) for i in range(ends)])  13.4 us
    div x6, other arithmetic, axis_flux(): (2.0 * relax_face * upwind + 0.5 * time_step * temp_face) / (2.0 * relax_...  11.4 us
  transfers between devices with their start and end apart: 25, of which 19 were waited for; matrix products, arithmetic and copies ran while one was open for 4% of the time, Pallas kernels for 0%

profile of v1, /device:TPU:0, one launch (start us, length us, event | category | flops | bytes accessed | tf_op | source)
XLA Modules:
  0.0 330.0 jit_solution(4430188509595245523)
XLA Ops:
  7.2 2.0 reduce_sum.36
  12.2 56.1 %all-reduce.12.cloned.1.call-done = f32[32,4,128]{2,1,0:T(4,128)} async-done(((f32[32,4,128]{2,1,0:T(4,128)}), f32[32,4,128]{2,1,0:T(4,128)}) %all-reduce.12.cloned.1.call-update) | async-done | bytes 65552 | tf_op jit(solution)/shard_map/psum | solution.py:167
  71.5 2.4 add_divide_fusion.1
  74.3 3.4 %collective-permute-start = (f32[34,2,4,128]{3,1,2,0:T(2,128)S(1)}, f32[34,2,4,128]{3,1,2,0:T(2,128)S(1)}, u32[]{:S(2)}, u32[]{:S(2)}) collective-permute-start(f32[34,2,4,128]{3,1,2,0:T(2,128)S(1)} %get-tuple-element.44), channel_id=1, source_target_pairs={{0,2},{1,3},{4,6},{5,7},{8,10},{9,11},{12,14},{13,15},{16,18},{17,... | collective-permute-start | bytes 417800 | tf_op jit(solution)/shard_map/ppermute | solution.py:24
  79.0 2.6 fusion.4
  81.5 3.0 collective-permute-done.1
  85.2 3.5 %collective-permute-start.2 = (f32[34,36,2,128]{3,1,2,0:T(8,128)S(1)}, f32[34,36,2,128]{3,1,2,0:T(8,128)S(1)}, u32[]{:S(2)}, u32[]{:S(2)}) collective-permute-start(f32[34,36,2,128]{3,1,2,0:T(8,128)S(1)} %get-tuple-element.33), channel_id=1, source_target_pairs={{0,1},{2,3},{4,5},{6,7},{8,9},{10,11},{12,13},{14,15},{16,17},{18,... | collective-permute-start | bytes 3760136 | tf_op jit(solution)/shard_map/ppermute | solution.py:24
  88.7 1.5 collective-permute-start.3
  92.2 1.4 fusion.66
  93.6 21.6 %collective-permute-done.2 = f32[34,36,2,128]{3,1,2,0:T(8,128)S(1)} collective-permute-done((f32[34,36,2,128]{3,1,2,0:T(8,128)S(1)}, f32[34,36,2,128]{3,1,2,0:T(8,128)S(1)}, u32[]{:S(2)}, u32[]{:S(2)}) %collective-permute-start.2) | collective-permute-done | bytes 1253408 | tf_op jit(solution)/shard_map/ppermute | solution.py:24
  115.3 4.2 %collective-permute-done.3 = f32[34,36,2,128]{3,1,2,0:T(8,128)S(1)} collective-permute-done((f32[34,36,2,128]{3,1,2,0:T(8,128)S(1)}, f32[34,36,2,128]{3,1,2,0:T(8,128)S(1)}, u32[]{:S(2)}, u32[]{:S(2)}) %collective-permute-start.3) | collective-permute-done | bytes 1253408 | tf_op jit(solution)/shard_map/ppermute | solution.py:26
  119.5 3.6 %fusion.18 = (f32[34,36,6,128]{3,1,2,0:T(8,128)S(1)}, f32[34,36,6,128]{3,1,2,0:T(8,128)S(1)}) fusion(f32[1,32,4,128]{3,1,2,0:T(8,128)S(1)} %bitcast.71, f32[34,36,2,128]{3,1,2,0:T(8,128)S(1)} %collective-permute-done.3, f32[34,2,4,128]{3,1,2,0:T(2,128)S(1)} %collective-permute-done.1, f32[1,32,4,128]{3,1,2,0:T(8,128)S(1)} %copy.44, ...), kind=kLoop, calls=%fused_computation.41 | loop fusion | flops 9400320 | bytes 12533760 | tf_op jit(solution)/shard_map/concatenate | solution.py:22
  123.1 3.5 %add_divide_fusion.3 = f32[32,32,6,128]{3,1,2,0:T(8,128)S(1)} fusion(f32[34,36,6,128]{3,1,2,0:T(8,128)S(1)} %get-tuple-element.37, f32[34,36,6,128]{3,1,2,0:T(8,128)S(1)} %get-tuple-element.36, f32[34,36,2,128]{3,1,2,0:T(8,128)S(1)} %collective-permute-done.3, f32[34,2,4,128]{3,1,2,0:T(2,128)S(1)} %collective-permute-done.1, ...), kind=kLoop, calls=%fused_computation.74 | loop fusion | flops 14155776 | bytes 14450688 | tf_op jit(solution)/shard_map/div | solution.py:63
  126.6 1.7 fusion.60
  128.4 1.8 fusion.159
  130.9 53.1 %all-reduce.14.cloned.1.call-done = f32[32,4,128]{2,1,0:T(4,128)} async-done(((f32[32,4,128]{2,1,0:T(4,128)}), f32[32,4,128]{2,1,0:T(4,128)}) %all-reduce.14.cloned.1.call-update) | async-done | bytes 65552 | tf_op jit(solution)/shard_map/psum | solution.py:167
  187.1 2.4 add_divide_fusion
  189.8 3.4 %collective-permute-start.4 = (f32[34,2,4,128]{3,1,2,0:T(2,128)S(1)}, f32[34,2,4,128]{3,1,2,0:T(2,128)S(1)}, u32[]{:S(2)}, u32[]{:S(2)}) collective-permute-start(f32[34,2,4,128]{3,1,2,0:T(2,128)S(1)} %get-tuple-element.40), channel_id=1, source_target_pairs={{0,2},{1,3},{4,6},{5,7},{8,10},{9,11},{12,14},{13,15},{16,18},{17,... | collective-permute-start | bytes 417800 | tf_op jit(solution)/shard_map/ppermute | solution.py:24
  193.2 1.3 collective-permute-start.5
  194.6 2.6 fusion.12
  197.1 3.0 collective-permute-done.5
  200.8 3.7 %collective-permute-start.6 = (f32[34,36,2,128]{3,1,2,0:T(8,128)S(1)}, f32[34,36,2,128]{3,1,2,0:T(8,128)S(1)}, u32[]{:S(2)}, u32[]{:S(2)}) collective-permute-start(f32[34,36,2,128]{3,1,2,0:T(8,128)S(1)} %get-tuple-element.31), channel_id=1, source_target_pairs={{0,1},{2,3},{4,5},{6,7},{8,9},{10,11},{12,13},{14,15},{16,17},{18,... | collective-permute-start | bytes 3760136 | tf_op jit(solution)/shard_map/ppermute | solution.py:24
  204.5 1.3 collective-permute-start.7
  207.8 1.4 fusion.54
  209.3 21.8 %collective-permute-done.6 = f32[34,36,2,128]{3,1,2,0:T(8,128)S(1)} collective-permute-done((f32[34,36,2,128]{3,1,2,0:T(8,128)S(1)}, f32[34,36,2,128]{3,1,2,0:T(8,128)S(1)}, u32[]{:S(2)}, u32[]{:S(2)}) %collective-permute-start.6) | collective-permute-done | bytes 1253408 | tf_op jit(solution)/shard_map/ppermute | solution.py:24
  231.1 4.2 %collective-permute-done.7 = f32[34,36,2,128]{3,1,2,0:T(8,128)S(1)} collective-permute-done((f32[34,36,2,128]{3,1,2,0:T(8,128)S(1)}, f32[34,36,2,128]{3,1,2,0:T(8,128)S(1)}, u32[]{:S(2)}, u32[]{:S(2)}) %collective-permute-start.7) | collective-permute-done | bytes 1253408 | tf_op jit(solution)/shard_map/ppermute | solution.py:26
  235.3 3.6 %fusion.21 = (f32[34,36,6,128]{3,1,2,0:T(8,128)S(1)}, f32[34,36,6,128]{3,1,2,0:T(8,128)S(1)}) fusion(f32[1,32,4,128]{3,1,2,0:T(8,128)S(1)} %bitcast.76, f32[34,36,2,128]{3,1,2,0:T(8,128)S(1)} %collective-permute-done.7, f32[34,2,4,128]{3,1,2,0:T(2,128)S(1)} %collective-permute-done.5, f32[1,32,4,128]{3,1,2,0:T(8,128)S(1)} %copy.48, ...), kind=kLoop, calls=%fused_computation.44 | loop fusion | flops 9400320 | bytes 12533760 | tf_op jit(solution)/shard_map/concatenate | solution.py:22
  238.9 3.5 %add_divide_fusion.2 = f32[32,32,6,128]{3,1,2,0:T(8,128)S(1)} fusion(f32[34,36,6,128]{3,1,2,0:T(8,128)S(1)} %get-tuple-element.35, f32[34,36,6,128]{3,1,2,0:T(8,128)S(1)} %get-tuple-element.34, f32[34,36,2,128]{3,1,2,0:T(8,128)S(1)} %collective-permute-done.7, f32[34,2,4,128]{3,1,2,0:T(2,128)S(1)} %collective-permute-done.5, ...), kind=kLoop, calls=%fused_computation.73 | loop fusion | flops 14155776 | bytes 14450688 | tf_op jit(solution)/shard_map/div | solution.py:63
  242.4 1.7 fusion.48
  244.2 1.8 fusion.157
  246.9 1.5 collective-permute-done.8
  249.5 7.5 %collective-permute-done.9 = f32[4,32,4,128]{3,2,1,0:T(4,128)S(1)} collective-permute-done((f32[4,32,4,128]{3,2,1,0:T(4,128)S(1)}, f32[4,32,4,128]{3,2,1,0:T(4,128)S(1)}, u32[]{:S(2)}, u32[]{:S(2)}) %collective-permute-start.9) | collective-permute-done | bytes 262176 | tf_op jit(solution)/shard_map/ppermute | solution.py:184
  258.3 12.8 %collective-permute-done.10 = f32[4,32,4,128]{3,2,1,0:T(4,128)S(1)} collective-permute-done((f32[4,32,4,128]{3,2,1,0:T(4,128)S(1)}, f32[4,32,4,128]{3,2,1,0:T(4,128)S(1)}, u32[]{:S(2)}, u32[]{:S(2)}) %collective-permute-start.10) | collective-permute-done | bytes 262176 | tf_op jit(solution)/shard_map/ppermute | solution.py:184
  271.2 2.4 collective-permute-start.11
  274.9 4.2 %collective-permute-done.12 = f32[3,1,4,128]{3,2,1,0:T(4,128)S(1)} collective-permute-done((f32[3,1,4,128]{3,2,1,0:T(4,128)S(1)}, f32[3,1,4,128]{3,2,1,0:T(4,128)S(1)}, u32[]{:S(2)}, u32[]{:S(2)}) %collective-permute-start.12) | collective-permute-done | bytes 6176 | tf_op jit(solution)/shard_map/ppermute | solution.py:26
  279.2 1.5 collective-permute-start.13
  282.4 4.3 %collective-permute-done.14 = f32[3,34,1,128]{3,2,1,0:T(1,128)S(1)} collective-permute-done((f32[3,34,1,128]{3,2,1,0:T(1,128)S(1)}, f32[3,34,1,128]{3,2,1,0:T(1,128)S(1)}, u32[]{:S(2)}, u32[]{:S(2)}) %collective-permute-start.14) | collective-permute-done | bytes 52256 | tf_op jit(solution)/shard_map/ppermute | solution.py:26
  288.2 1.6 collective-permute-start.15
  289.8 1.3 collective-permute-start.16
  291.1 4.2 %collective-permute-done.16 = f32[1,1,4,128]{3,2,1,0:T(4,128)S(1)} collective-permute-done((f32[1,1,4,128]{3,2,1,0:T(4,128)S(1)}, f32[1,1,4,128]{3,2,1,0:T(4,128)S(1)}, u32[]{:S(2)}, u32[]{:S(2)}) %collective-permute-start.16) | collective-permute-done | bytes 2080 | tf_op jit(solution)/shard_map/ppermute | solution.py:26
  295.3 1.6 collective-permute-start.17
  296.9 1.6 collective-permute-start.18
  298.5 4.1 %collective-permute-done.18 = f32[1,34,1,128]{3,2,1,0:T(1,128)S(1)} collective-permute-done((f32[1,34,1,128]{3,2,1,0:T(1,128)S(1)}, f32[1,34,1,128]{3,2,1,0:T(1,128)S(1)}, u32[]{:S(2)}, u32[]{:S(2)}) %collective-permute-start.18) | collective-permute-done | bytes 17440 | tf_op jit(solution)/shard_map/ppermute | solution.py:26
  303.6 1.7 collective-permute-start.19
  306.6 4.2 %collective-permute-done.20 = f32[1,1,4,128]{3,2,1,0:T(4,128)S(1)} collective-permute-done((f32[1,1,4,128]{3,2,1,0:T(4,128)S(1)}, f32[1,1,4,128]{3,2,1,0:T(4,128)S(1)}, u32[]{:S(2)}, u32[]{:S(2)}) %collective-permute-start.20) | collective-permute-done | bytes 2080 | tf_op jit(solution)/shard_map/ppermute | solution.py:26
  310.8 1.6 collective-permute-start.21
  313.9 4.2 %collective-permute-done.22 = f32[1,34,1,128]{3,2,1,0:T(1,128)S(1)} collective-permute-done((f32[1,34,1,128]{3,2,1,0:T(1,128)S(1)}, f32[1,34,1,128]{3,2,1,0:T(1,128)S(1)}, u32[]{:S(2)}, u32[]{:S(2)}) %collective-permute-start.22) | collective-permute-done | bytes 17440 | tf_op jit(solution)/shard_map/ppermute | solution.py:26
  320.1 3.1 copy.53
  (96 shorter events, 31.0 us)
Async XLA Ops:
  7.2 63.9 %copy-start = (f32[32,32,4,128]{3,2,1,0:T(4,128)S(1)}, f32[32,32,4,128]{3,2,1,0:T(4,128)}, u32[]{:S(2)}) copy-start(f32[32,32,4,128]{3,2,1,0:T(4,128)} %param.2) | copy-start | bytes 6291460
  7.2 61.1 %all-reduce.12.cloned.1.call-start = ((), (), s32[]{:S(2)}) async-start(), calls=%async_computation | async-start | bytes 131072 | tf_op jit(solution)/shard_map/psum | solution.py:167
  9.9 174.0 %all-reduce.14.cloned.1.call-start = ((), (), s32[]{:S(2)}) async-start(), calls=%async_computation.1 | async-start | bytes 131072 | tf_op jit(solution)/shard_map/psum | solution.py:167
  74.3 7.3 %collective-permute-start = (f32[34,2,4,128]{3,1,2,0:T(2,128)S(1)}, f32[34,2,4,128]{3,1,2,0:T(2,128)S(1)}, u32[]{:S(2)}, u32[]{:S(2)}) collective-permute-start(f32[34,2,4,128]{3,1,2,0:T(2,128)S(1)} %get-tuple-element.44), channel_id=1, source_target_pairs={{0,2},{1,3},{4,6},{5,7},{8,10},{9,11},{12,14},{13,15},{16,18},{17,... | collective-permute-start | bytes 417800 | tf_op jit(solution)/shard_map/ppermute | solution.py:24
  77.6 6.9 %collective-permute-start.1 = (f32[34,2,4,128]{3,1,2,0:T(2,128)S(1)}, f32[34,2,4,128]{3,1,2,0:T(2,128)S(1)}, u32[]{:S(2)}, u32[]{:S(2)}) collective-permute-start(f32[34,2,4,128]{3,1,2,0:T(2,128)S(1)} %get-tuple-element.45), channel_id=1, source_target_pairs={{2,0},{3,1},{6,4},{7,5},{10,8},{11,9},{14,12},{15,13},{18,16},{19,... | collective-permute-start | bytes 417800 | tf_op jit(solution)/shard_map/ppermute | solution.py:26
  85.2 30.0 %collective-permute-start.2 = (f32[34,36,2,128]{3,1,2,0:T(8,128)S(1)}, f32[34,36,2,128]{3,1,2,0:T(8,128)S(1)}, u32[]{:S(2)}, u32[]{:S(2)}) collective-permute-start(f32[34,36,2,128]{3,1,2,0:T(8,128)S(1)} %get-tuple-element.33), channel_id=1, source_target_pairs={{0,1},{2,3},{4,5},{6,7},{8,9},{10,11},{12,13},{14,15},{16,17},{18,... | collective-permute-start | bytes 3760136 | tf_op jit(solution)/shard_map/ppermute | solution.py:24
  88.7 30.7 %collective-permute-start.3 = (f32[34,36,2,128]{3,1,2,0:T(8,128)S(1)}, f32[34,36,2,128]{3,1,2,0:T(8,128)S(1)}, u32[]{:S(2)}, u32[]{:S(2)}) collective-permute-start(f32[34,36,2,128]{3,1,2,0:T(8,128)S(1)} %get-tuple-element.32), channel_id=1, source_target_pairs={{1,0},{3,2},{5,4},{7,6},{9,8},{11,10},{13,12},{15,14},{17,16},{19,... | collective-permute-start | bytes 3760136 | tf_op jit(solution)/shard_map/ppermute | solution.py:26
  126.6 1.8 copy-start.1
  189.8 7.3 %collective-permute-start.4 = (f32[34,2,4,128]{3,1,2,0:T(2,128)S(1)}, f32[34,2,4,128]{3,1,2,0:T(2,128)S(1)}, u32[]{:S(2)}, u32[]{:S(2)}) collective-permute-start(f32[34,2,4,128]{3,1,2,0:T(2,128)S(1)} %get-tuple-element.40), channel_id=1, source_target_pairs={{0,2},{1,3},{4,6},{5,7},{8,10},{9,11},{12,14},{13,15},{16,18},{17,... | collective-permute-start | bytes 417800 | tf_op jit(solution)/shard_map/ppermute | solution.py:24
  193.2 6.9 %collective-permute-start.5 = (f32[34,2,4,128]{3,1,2,0:T(2,128)S(1)}, f32[34,2,4,128]{3,1,2,0:T(2,128)S(1)}, u32[]{:S(2)}, u32[]{:S(2)}) collective-permute-start(f32[34,2,4,128]{3,1,2,0:T(2,128)S(1)} %get-tuple-element.41), channel_id=1, source_target_pairs={{2,0},{3,1},{6,4},{7,5},{10,8},{11,9},{14,12},{15,13},{18,16},{19,... | collective-permute-start | bytes 417800 | tf_op jit(solution)/shard_map/ppermute | solution.py:26
  200.8 30.2 %collective-permute-start.6 = (f32[34,36,2,128]{3,1,2,0:T(8,128)S(1)}, f32[34,36,2,128]{3,1,2,0:T(8,128)S(1)}, u32[]{:S(2)}, u32[]{:S(2)}) collective-permute-start(f32[34,36,2,128]{3,1,2,0:T(8,128)S(1)} %get-tuple-element.31), channel_id=1, source_target_pairs={{0,1},{2,3},{4,5},{6,7},{8,9},{10,11},{12,13},{14,15},{16,17},{18,... | collective-permute-start | bytes 3760136 | tf_op jit(solution)/shard_map/ppermute | solution.py:24
  204.5 30.7 %collective-permute-start.7 = (f32[34,36,2,128]{3,1,2,0:T(8,128)S(1)}, f32[34,36,2,128]{3,1,2,0:T(8,128)S(1)}, u32[]{:S(2)}, u32[]{:S(2)}) collective-permute-start(f32[34,36,2,128]{3,1,2,0:T(8,128)S(1)} %get-tuple-element.30), channel_id=1, source_target_pairs={{1,0},{3,2},{5,4},{7,6},{9,8},{11,10},{13,12},{15,14},{17,16},{19,... | collective-permute-start | bytes 3760136 | tf_op jit(solution)/shard_map/ppermute | solution.py:26
  246.8 1.6 collective-permute-start.8
  248.5 8.4 %collective-permute-start.9 = (f32[4,32,4,128]{3,2,1,0:T(4,128)S(1)}, f32[4,32,4,128]{3,2,1,0:T(4,128)S(1)}, u32[]{:S(2)}, u32[]{:S(2)}) collective-permute-start(f32[4,32,4,128]{3,2,1,0:T(4,128)S(1)} %fusion.154), channel_id=1, source_target_pairs={{0,8},{4,12},{8,0},{12,4},{16,24},{20,28},{24,16},{28,20},{1,9},{5... | collective-permute-start | bytes 786440 | tf_op jit(solution)/shard_map/ppermute | solution.py:184
  257.0 14.1 %collective-permute-start.10 = (f32[4,32,4,128]{3,2,1,0:T(4,128)S(1)}, f32[4,32,4,128]{3,2,1,0:T(4,128)S(1)}, u32[]{:S(2)}, u32[]{:S(2)}) collective-permute-start(f32[4,32,4,128]{3,2,1,0:T(4,128)S(1)} %add.694), channel_id=1, source_target_pairs={{0,16},{4,20},{8,24},{12,28},{16,0},{20,4},{24,8},{28,12},{1,17},{... | collective-permute-start | bytes 786440 | tf_op jit(solution)/shard_map/ppermute | solution.py:184
  271.2 3.7 %collective-permute-start.11 = (f32[3,1,4,128]{3,2,1,0:T(4,128)S(1)}, f32[3,1,4,128]{3,2,1,0:T(4,128)S(1)}, u32[]{:S(2)}, u32[]{:S(2)}) collective-permute-start(f32[3,1,4,128]{3,2,1,0:T(4,128)S(1)} %get-tuple-element.49), channel_id=1, source_target_pairs={{0,2},{1,3},{4,6},{5,7},{8,10},{9,11},{12,14},{13,15},{16,18},{17,... | collective-permute-start | bytes 18440 | tf_op jit(solution)/shard_map/ppermute | solution.py:24
  273.6 5.5 %collective-permute-start.12 = (f32[3,1,4,128]{3,2,1,0:T(4,128)S(1)}, f32[3,1,4,128]{3,2,1,0:T(4,128)S(1)}, u32[]{:S(2)}, u32[]{:S(2)}) collective-permute-start(f32[3,1,4,128]{3,2,1,0:T(4,128)S(1)} %get-tuple-element.50), channel_id=1, source_target_pairs={{2,0},{3,1},{6,4},{7,5},{10,8},{11,9},{14,12},{15,13},{18,16},{19,... | collective-permute-start | bytes 18440 | tf_op jit(solution)/shard_map/ppermute | solution.py:26
  279.2 3.2 collective-permute-start.13
  280.7 6.0 %collective-permute-start.14 = (f32[3,34,1,128]{3,2,1,0:T(1,128)S(1)}, f32[3,34,1,128]{3,2,1,0:T(1,128)S(1)}, u32[]{:S(2)}, u32[]{:S(2)}) collective-permute-start(f32[3,34,1,128]{3,2,1,0:T(1,128)S(1)} %get-tuple-element.52), channel_id=1, source_target_pairs={{1,0},{3,2},{5,4},{7,6},{9,8},{11,10},{13,12},{15,14},{17,16},{19,... | collective-permute-start | bytes 156680 | tf_op jit(solution)/shard_map/ppermute | solution.py:26
  288.2 3.0 collective-permute-start.15
  289.8 5.5 %collective-permute-start.16 = (f32[1,1,4,128]{3,2,1,0:T(4,128)S(1)}, f32[1,1,4,128]{3,2,1,0:T(4,128)S(1)}, u32[]{:S(2)}, u32[]{:S(2)}) collective-permute-start(f32[1,1,4,128]{3,2,1,0:T(4,128)S(1)} %get-tuple-element.60), channel_id=1, source_target_pairs={{2,0},{3,1},{6,4},{7,5},{10,8},{11,9},{14,12},{15,13},{18,16},{19,... | collective-permute-start | bytes 6152 | tf_op jit(solution)/shard_map/ppermute | solution.py:26
  295.3 3.2 collective-permute-start.17
  296.9 5.6 %collective-permute-start.18 = (f32[1,34,1,128]{3,2,1,0:T(1,128)S(1)}, f32[1,34,1,128]{3,2,1,0:T(1,128)S(1)}, u32[]{:S(2)}, u32[]{:S(2)}) collective-permute-start(f32[1,34,1,128]{3,2,1,0:T(1,128)S(1)} %get-tuple-element.56), channel_id=1, source_target_pairs={{1,0},{3,2},{5,4},{7,6},{9,8},{11,10},{13,12},{15,14},{17,16},{19,... | collective-permute-start | bytes 52232 | tf_op jit(solution)/shard_map/ppermute | solution.py:26
  303.6 3.0 collective-permute-start.19
  305.3 5.5 %collective-permute-start.20 = (f32[1,1,4,128]{3,2,1,0:T(4,128)S(1)}, f32[1,1,4,128]{3,2,1,0:T(4,128)S(1)}, u32[]{:S(2)}, u32[]{:S(2)}) collective-permute-start(f32[1,1,4,128]{3,2,1,0:T(4,128)S(1)} %get-tuple-element.58), channel_id=1, source_target_pairs={{2,0},{3,1},{6,4},{7,5},{10,8},{11,9},{14,12},{15,13},{18,16},{19,... | collective-permute-start | bytes 6152 | tf_op jit(solution)/shard_map/ppermute | solution.py:26
  310.8 3.1 collective-permute-start.21
  312.5 5.6 %collective-permute-start.22 = (f32[1,34,1,128]{3,2,1,0:T(1,128)S(1)}, f32[1,34,1,128]{3,2,1,0:T(1,128)S(1)}, u32[]{:S(2)}, u32[]{:S(2)}) collective-permute-start(f32[1,34,1,128]{3,2,1,0:T(1,128)S(1)} %get-tuple-element.54), channel_id=1, source_target_pairs={{1,0},{3,2},{5,4},{7,6},{9,8},{11,10},{13,12},{15,14},{17,16},{19,... | collective-permute-start | bytes 52232 | tf_op jit(solution)/shard_map/ppermute | solution.py:26
Sparse Core Ops, SparseCore 0:
  10.9 57.4 all-reduce.11
  131.0 52.9 all-reduce.13
